TPU v7x, 768 devices: a whole 4x8x12 slice. The times are simulated.
768 devices in a mesh: section: 24 (over z_lo, x, core), seq: 32 (over z_hi, y).
Axes of the slice: x: 4, y: 8, z: 12 (z_hi: 4, z_lo: 3; z = z_hi * 3 + z_lo), core: 2. Of those that a mesh axis runs over, the one named last changes fastest.
Arguments:
- queries: bfloat16 [8192, 3072], P('seq', 'section'), may hold values from -64 to 64
- key_rows: bfloat16 [8192, 3072], P('seq', 'section'), may hold values from -64 to 64
- values: bfloat16 [8192, 3072], P('seq', 'section'), may hold values from -6 to 6
- out_grad: bfloat16 [8192, 3072], P('seq', 'section'), may hold values from -6 to 6
- query_gain: float32 [3072], P('section'), may hold values from 1 to 3
- key_gain: float32 [3072], P('section'), may hold values from 1 to 3
- stretch_id: int32 [8192], P('seq'), may hold values from 0 to 31, as said below
Outputs:
- attended: bfloat16 [8192, 3072], P('seq', 'section')
- grad_queries: float32 [8192, 3072], P('seq', 'section')
- grad_keys: float32 [8192, 3072], P('seq', 'section')
- grad_values: float32 [8192, 3072], P('seq', 'section')
Inputs may be any that keep to these rules, and one draw needn't show every extreme that they name: stretch_id never falls along the tokens and changes only at multiples of 128 tokens (whole latent frames); the first frame is stretch 0 alone, stretch 1 spans exactly three frames (384 tokens); from frame 4 on, stretches come in consecutive pairs that together span exactly four frames, each stretch one to three frames.
All inputs are finite; a program needn't handle non-finite values.
Results may differ from a plain program's by a relative error of at most 0.038.
Values may be sent and summed in bfloat16 or wider, within the bound.
No kernel may reach another device: no remote copies, remote signals or barrier semaphores. Data moves between devices by JAX's collectives and lax.ppermute only.
A program may use at most 32 MiB of HBM per device.

v0:
```python
import math

import jax
import jax.numpy as jnp
from jax import lax
from jax.sharding import PartitionSpec as P

EPSILON = 1e-06
NEG_FILL = -1e30


def block_length(row_count, shard_rows):
    per_block = max(1, 1024 // shard_rows)
    while row_count % (per_block * shard_rows) != 0:
        per_block = per_block - 1
    return per_block * shard_rows


def in_blocks(shard_piece, shard_rows):
    length = block_length(shard_piece[0].shape[0], shard_rows)
    return jax.tree.map(
        lambda member: member.reshape((member.shape[0] // length, length) + member.shape[1:]),
        shard_piece,
    )


def on_device(queries, key_rows, values, out_grad, query_gain, key_gain, stretch_id):
    shard_rows, head_size = queries.shape
    width = head_size * lax.axis_size("section")
    score_scale = 1.0 / math.sqrt(head_size)
    query_wide = queries.astype(jnp.float32)
    key_wide = key_rows.astype(jnp.float32)
    squares = lax.psum(
        (jnp.sum(query_wide * query_wide, axis=1), jnp.sum(key_wide * key_wide, axis=1)), "section"
    )
    query_root = lax.rsqrt(squares[0] / width + EPSILON)
    key_root = lax.rsqrt(squares[1] / width + EPSILON)
    query_hat = (query_wide * query_root[:, None] * query_gain[None, :]).astype(jnp.bfloat16)
    key_hat = (key_wide * key_root[:, None] * key_gain[None, :]).astype(jnp.bfloat16)

    def forward_block(carried, key_block):
        key_part, value_part, stretch_part = key_block
        accumulated, run_top, run_sum = carried
        scores = (
            jnp.einsum("td,ud->tu", query_hat, key_part, preferred_element_type=jnp.float32)
            * score_scale
        )
        visible = stretch_part[None, :] <= stretch_id[:, None]
        scores = jnp.where(visible, scores, NEG_FILL)
        new_top = jnp.maximum(run_top, jnp.max(scores, axis=1))
        weights = jnp.exp(scores - new_top[:, None])
        factor = jnp.exp(run_top - new_top)
        accumulated = accumulated * factor[:, None] + jnp.dot(
            weights.astype(jnp.bfloat16), value_part, preferred_element_type=jnp.float32
        )
        return ((accumulated, new_top, run_sum * factor + jnp.sum(weights, axis=1)), None)

    zero_rows = jnp.zeros((shard_rows, head_size), jnp.float32)
    initial = (
        zero_rows,
        jnp.full((shard_rows,), NEG_FILL, jnp.float32),
        jnp.zeros((shard_rows,), jnp.float32),
    )
    result, _ = lax.scan(
        forward_block,
        initial,
        in_blocks(
            (
                lax.all_gather(key_hat, "seq", axis=0, tiled=True),
                lax.all_gather(values, "seq", axis=0, tiled=True),
                lax.all_gather(stretch_id, "seq", axis=0, tiled=True),
            ),
            shard_rows,
        ),
    )
    accumulated, run_top, run_sum = result
    attended = (accumulated / run_sum[:, None]).astype(jnp.bfloat16)
    log_total = run_top + jnp.log(run_sum)
    row_delta = jnp.sum(out_grad.astype(jnp.float32) * attended.astype(jnp.float32), axis=1)

    def query_side_update(query_grad, key_block):
        key_part, value_part, stretch_part = key_block
        scores = (
            jnp.einsum("td,ud->tu", query_hat, key_part, preferred_element_type=jnp.float32)
            * score_scale
        )
        visible = stretch_part[None, :] <= stretch_id[:, None]
        chances = jnp.exp(jnp.where(visible, scores, NEG_FILL) - log_total[:, None])
        grad_chances = jnp.einsum(
            "td,ud->tu", out_grad, value_part, preferred_element_type=jnp.float32
        )
        grad_scores = (chances * (grad_chances - row_delta[:, None])).astype(jnp.bfloat16)
        return (
            query_grad
            + jnp.dot(grad_scores, key_part, preferred_element_type=jnp.float32) * score_scale
        )

    def key_side_update(grad_pair, query_block):
        query_part, grad_part, total_part, delta_part, stretch_part = query_block
        key_grad, value_grad = grad_pair
        scores = (
            jnp.einsum("td,ud->tu", query_part, key_hat, preferred_element_type=jnp.float32)
            * score_scale
        )
        visible = stretch_id[None, :] <= stretch_part[:, None]
        chances = jnp.exp(jnp.where(visible, scores, NEG_FILL) - total_part[:, None])
        grad_chances = jnp.einsum(
            "td,ud->tu", grad_part, values, preferred_element_type=jnp.float32
        )
        grad_scores = (chances * (grad_chances - delta_part[:, None])).astype(jnp.bfloat16)
        key_grad = (
            key_grad
            + jnp.einsum("tu,td->ud", grad_scores, query_part, preferred_element_type=jnp.float32)
            * score_scale
        )
        value_grad = value_grad + jnp.einsum(
            "tu,td->ud", chances.astype(jnp.bfloat16), grad_part, preferred_element_type=jnp.float32
        )
        return (key_grad, value_grad)

    def query_step(current, key_block):
        return (query_side_update(current, key_block), None)

    result, _ = lax.scan(
        query_step,
        zero_rows,
        in_blocks(
            (
                lax.all_gather(key_hat, "seq", axis=0, tiled=True),
                lax.all_gather(values, "seq", axis=0, tiled=True),
                lax.all_gather(stretch_id, "seq", axis=0, tiled=True),
            ),
            shard_rows,
        ),
    )
    query_grad = result

    def key_step(current, query_block):
        return (key_side_update(current, query_block), None)

    result, _ = lax.scan(
        key_step,
        (zero_rows, zero_rows),
        in_blocks(
            (
                lax.all_gather(query_hat.astype(jnp.float32), "seq", axis=0, tiled=True).astype(
                    jnp.bfloat16
                ),
                lax.all_gather(out_grad.astype(jnp.float32), "seq", axis=0, tiled=True).astype(
                    jnp.bfloat16
                ),
                lax.all_gather(log_total, "seq", axis=0, tiled=True),
                lax.all_gather(row_delta, "seq", axis=0, tiled=True),
                lax.all_gather(stretch_id, "seq", axis=0, tiled=True),
            ),
            shard_rows,
        ),
    )
    key_grad, value_grad = result
    totals = lax.psum(
        (
            jnp.sum(query_grad * query_gain[None, :] * query_wide, axis=1),
            jnp.sum(key_grad * key_gain[None, :] * key_wide, axis=1),
        ),
        "section",
    )
    grad_queries = (
        query_gain[None, :] * query_root[:, None] * query_grad
        - query_wide * (query_root**3 * totals[0] / width)[:, None]
    )
    grad_keys = (
        key_gain[None, :] * key_root[:, None] * key_grad
        - key_wide * (key_root**3 * totals[1] / width)[:, None]
    )
    return (attended, grad_queries, grad_keys, value_grad)


def solution(mesh):
    placed = (
        P("seq", "section"),
        P("seq", "section"),
        P("seq", "section"),
        P("seq", "section"),
        P("section"),
        P("section"),
        P("seq"),
    )
    return jax.shard_map(
        on_device,
        mesh=mesh,
        in_specs=placed,
        out_specs=(
            P("seq", "section"),
            P("seq", "section"),
            P("seq", "section"),
            P("seq", "section"),
        ),
        check_vma=False,
    )
```

profile of v0, /device:TPU:1, one launch (start us, length us, event | category | flops | bytes accessed | tf_op | source)
XLA Modules:
  0.0 587.3 jit_solution(2614911659560226102)
XLA Ops:
  9.1 55.3 %all-reduce.1 = (f32[256]{0:T(256)S(1)}, f32[256]{0:T(256)S(1)}) all-reduce(f32[256]{0:T(256)S(1)} %fusion.60, f32[256]{0:T(256)S(1)} %fusion.65), channel_id=1, replica_groups=mesh['section'=24,'seq'=32] {'section'}, use_global_device_ids=true, to_apply=%region_1.0 | all-reduce | flops 512 | bytes 4096 | tf_op jit(solution)/shard_map/psum | solution.py:33
  64.4 1.6 fusion.62
  66.8 1.6 fusion.67
  69.1 75.6 %all-gather = s32[32,1,256]{2,1,0:T(1,128)S(1)} all-gather(s32[1,1,256]{2,1,0:T(1,128)} %bitcast.122), channel_id=1, replica_groups=mesh['section'=24,'seq'=32] {'seq'}, dimensions={0}, use_global_device_ids=true | all-gather | bytes 33792 | tf_op jit(solution)/shard_map/all_gather | solution.py:71
  144.8 27.0 %all-gather.8.cloned.1.call-done = bf16[8192,128]{1,0:T(8,128)(2,1)} async-done(((bf16[256,128]{1,0:T(8,128)(2,1)}), bf16[8192,128]{1,0:T(8,128)(2,1)}) %all-gather.8.cloned.1.call-update) | async-done | bytes 2097168 | tf_op jit(solution)/shard_map/all_gather | solution.py:69
  171.8 99.1 %all-gather.10.cloned.1.call-done = bf16[8192,128]{1,0:T(8,128)(2,1)} async-done(((bf16[256,128]{1,0:T(8,128)(2,1)}), bf16[8192,128]{1,0:T(8,128)(2,1)}) %all-gather.10.cloned.1.call-update) | async-done | bytes 2097168 | tf_op jit(solution)/shard_map/all_gather | solution.py:70
  270.9 23.7 %while.39 = (s32[]{:T(128)}, f32[256,128]{1,0:T(8,128)S(1)}, f32[256]{0:T(256)S(1)}, f32[256]{0:T(256)S(1)}, s32[8,1024]{1,0:T(8,128)S(1)}, /*index=5*/s32[256]{...) while((s32[]{:T(128)}, f32[256,128]{1,0:T(8,128)S(1)}, ...), condition=%wide.region_7.8_spmd.clone, body=%wide.region_4.7_spmd.clone.sunk | while | flops 136414464 | bytes 4028541 | solution.py:64
  295.4 76.0 %all-gather.2 = f32[32,1,256]{2,1,0:T(1,128)S(1)} all-gather(f32[1,1,256]{2,1,0:T(1,128)S(1)} %bitcast.120), channel_id=1, replica_groups=mesh['section'=24,'seq'=32] {'seq'}, dimensions={0}, use_global_device_ids=true | all-gather | bytes 33792 | tf_op jit(solution)/shard_map/all_gather | solution.py:153
  371.5 68.9 %all-gather.1 = f32[32,1,256]{2,1,0:T(1,128)S(1)} all-gather(f32[1,1,256]{2,1,0:T(1,128)S(1)} %bitcast.121), channel_id=1, replica_groups=mesh['section'=24,'seq'=32] {'seq'}, dimensions={0}, use_global_device_ids=true | all-gather | bytes 33792 | tf_op jit(solution)/shard_map/all_gather | solution.py:152
  440.5 23.6 %while.40 = (s32[]{:T(128)}, f32[256,128]{1,0:T(8,128)S(1)}, s32[8,1024]{1,0:T(8,128)S(1)}, s32[256]{0:T(256)}, bf16[8,1024,128]{2,1,0:T(8,128)(2,1)}, /*index=5...) while((s32[]{:T(128)}, f32[256,128]{1,0:T(8,128)S(1)}, ...), condition=%wide.region_10.11_spmd.clone, body=%wide.region_9.10_spmd.clone.sunk | while | flops 203259904 | bytes 3293827 | solution.py:124
  444.9 1.5 fusion.116
  447.8 1.5 fusion.116
  450.8 1.5 fusion.116
  464.2 8.5 %all-gather.14.cloned.1.call-done = bf16[8192,128]{1,0:T(8,128)(2,1)} async-done(((bf16[256,128]{1,0:T(8,128)(2,1)}), bf16[8192,128]{1,0:T(8,128)(2,1)}) %all-gather.14.cloned.1.call-update) | async-done | bytes 2097168 | tf_op jit(solution)/shard_map/all_gather | solution.py:149
  472.8 35.9 %while.41 = (s32[]{:T(128)}, f32[256,128]{1,0:T(8,128)S(1)}, f32[256,128]{1,0:T(8,128)S(1)}, s32[256]{0:T(256)}, s32[8,1024]{1,0:T(8,128)S(1)}, /*index=5*/bf16[...) while((s32[]{:T(128)}, f32[256,128]{1,0:T(8,128)S(1)}, ...), condition=%wide.region_14.15_spmd.clone, body=%wide.region_13.14_spmd.clone.sunk | while | flops 270696448 | bytes 4889744 | solution.py:141
  475.6 1.7 fusion.125
  480.0 1.7 fusion.125
  484.5 1.7 fusion.125
  489.0 1.7 fusion.125
  493.5 1.7 fusion.125
  498.0 1.7 fusion.125
  502.5 1.7 fusion.125
  507.0 1.7 fusion.125
  508.9 70.3 %all-reduce = (f32[256]{0:T(256)S(1)}, f32[256]{0:T(256)S(1)}) all-reduce(f32[256]{0:T(256)S(1)} %fusion.68, f32[256]{0:T(256)S(1)} %fusion.63), channel_id=1, replica_groups=mesh['section'=24,'seq'=32] {'section'}, use_global_device_ids=true, to_apply=%region_12.13 | all-reduce | flops 512 | bytes 4096 | tf_op jit(solution)/shard_map/psum | solution.py:160
  (157 shorter events, 69.9 us)
Async XLA Ops:
  7.2 164.6 %all-gather.8.cloned.1.call-start = ((), (), s32[]{:S(2)}) async-start(), calls=%async_computation | async-start | bytes 2162688 | tf_op jit(solution)/shard_map/all_gather | solution.py:69
  66.0 204.9 %all-gather.10.cloned.1.call-start = ((), (), s32[]{:S(2)}) async-start(), calls=%async_computation.1 | async-start | bytes 2162688 | tf_op jit(solution)/shard_map/all_gather | solution.py:70
  66.8 397.5 %all-gather.12.cloned.1.call-start = ((), (), s32[]{:S(2)}) async-start(), calls=%async_computation.2 | async-start | bytes 2162688 | tf_op jit(solution)/shard_map/all_gather | solution.py:146
  68.4 404.3 %all-gather.14.cloned.1.call-start = ((), (), s32[]{:S(2)}) async-start(), calls=%async_computation.3 | async-start | bytes 2162688 | tf_op jit(solution)/shard_map/all_gather | solution.py:149
  270.9 23.7 %copy-start.1 = (bf16[256,128]{1,0:T(8,128)(2,1)S(1)}, bf16[256,128]{1,0:T(8,128)(2,1)}, u32[]{:S(2)}) copy-start(bf16[256,128]{1,0:T(8,128)(2,1)} %param.16) | copy-start | bytes 196612
  440.5 23.6 %copy-start.4 = (bf16[256,128]{1,0:T(8,128)(2,1)S(1)}, bf16[256,128]{1,0:T(8,128)(2,1)}, u32[]{:S(2)}) copy-start(bf16[256,128]{1,0:T(8,128)(2,1)} %param.13) | copy-start | bytes 196612
  440.5 23.6 %copy-start.7 = (f32[128]{0:T(128)S(1)}, f32[128]{0:T(128)}, u32[]{:S(2)}) copy-start(f32[128]{0:T(128)} %param.17) | copy-start | bytes 1540
  440.5 32.3 %copy-start.2 = (bf16[256,128]{1,0:T(8,128)(2,1)S(1)}, bf16[256,128]{1,0:T(8,128)(2,1)}, u32[]{:S(2)}) copy-start(bf16[256,128]{1,0:T(8,128)(2,1)} %param.15) | copy-start | bytes 196612
  440.5 32.3 %copy-start.5 = (bf16[256,128]{1,0:T(8,128)(2,1)S(1)}, bf16[256,128]{1,0:T(8,128)(2,1)}, u32[]{:S(2)}) copy-start(bf16[256,128]{1,0:T(8,128)(2,1)} %fusion.62) | copy-start | bytes 196612
  472.8 36.0 %copy-start.3 = (bf16[256,128]{1,0:T(8,128)(2,1)S(1)}, bf16[256,128]{1,0:T(8,128)(2,1)}, u32[]{:S(2)}) copy-start(bf16[256,128]{1,0:T(8,128)(2,1)} %param.14) | copy-start | bytes 196612
  472.8 36.0 %copy-start.6 = (f32[128]{0:T(128)S(1)}, f32[128]{0:T(128)}, u32[]{:S(2)}) copy-start(f32[128]{0:T(128)} %param.18) | copy-start | bytes 1540
  508.7 72.0 %copy-start = (f32[256,128]{1,0:T(8,128)}, f32[256,128]{1,0:T(8,128)S(1)}, u32[]{:S(2)}) copy-start(f32[256,128]{1,0:T(8,128)S(1)} %get-tuple-element.162) | copy-start | bytes 393220
Sparse Core Ops, SparseCore 0:
  66.2 105.6 all-gather.7
  175.6 95.3 all-gather.9
  275.2 95.8 all-gather.11
  374.7 98.0 all-gather.13
where the time goes:
time: 594 us; the launch traced here: 587 us
  blocking collectives  346 us (58%)
  waiting for transfers between devices  136 us (23%)
  matrix products  79.7 us (13%)
  between operations  14 us (2%)
  other arithmetic  9.84 us (2%)
    all_gather x1, waiting for transfers between devices, on_device(): lax.all_gather(values, 'seq', axis=0, tiled=True)  99.1 us
    all_gather x1, blocking collectives, on_device(): lax.all_gather(row_delta, 'seq', axis=0, tiled=True)  76 us
    all_gather x1, blocking collectives, on_device(): lax.all_gather(stretch_id, 'seq', axis=0, tiled=True)  75.6 us
    psum x1, blocking collectives, on_device(): lax.psum((jnp.sum(query_grad * query_gain[None, :] * query_wide, axis=1),...  70.3 us
    all_gather x1, blocking collectives, on_device(): lax.all_gather(log_total, 'seq', axis=0, tiled=True)  68.9 us
    psum x1, blocking collectives, on_device(): lax.psum((jnp.sum(query_wide * query_wide, axis=1), jnp.sum(key_wide * ke...  55.3 us
    all_gather x1, waiting for transfers between devices, on_device(): lax.all_gather(key_hat, 'seq', axis=0, tiled=True)  27 us
    dot_general x8, matrix products, key_side_update(): jnp.einsum('tu,td->ud', grad_scores, query_part, preferred_element_type=j...  13.8 us
  transfers between devices with their start and end apart: 4, of which 3 were waited for; matrix products, arithmetic and copies ran while one was open for 8% of the time, Pallas kernels for 0%

commit v1 on v0

v1 whole, which is shorter than its diff:
```python
import math

import jax
import jax.numpy as jnp
from jax import lax
from jax.experimental import pallas as pl
from jax.experimental.pallas import tpu as pltpu
from jax.sharding import Mesh, PartitionSpec as P

EPSILON = 1e-06
NEG_FILL = -1e30
FLOOR = -1e20
LOG2E = 1.4426950408889634
SECTION = ("z_lo", "x", "core")
SEQ = ("z_hi", "y")
EXTRA = 16
NT = (((1,), (1,)), ((), ()))
NN = (((1,), (0,)), ((), ()))
TN = (((0,), (0,)), ((), ()))


def dot(a, b, dims):
    return lax.dot_general(a, b, dims, preferred_element_type=jnp.float32)


def forward_kernel(zh_ref, qd_ref, kv_ref, sid_ref, p_ref, o_ref, st_ref):
    rows = sid_ref.shape[0]
    dim = o_ref.shape[1]
    groups = kv_ref.shape[0]
    base = LOG2E / math.sqrt(dim)
    zh = zh_ref[0]
    q = qd_ref[0, :rows, :dim]
    do = qd_ref[0, :rows, dim:]
    sid_q = qd_ref[0, rows : rows + EXTRA, :][:1, :].astype(jnp.float32)
    hidden = sid_ref[:, :1] > sid_q

    def run(count):
        parts = []
        top = None
        for b in range(count):
            s = dot(kv_ref[b, :, :dim], q, NT)
            if b == count - 1:
                s = jnp.where(hidden, NEG_FILL, s)
            parts.append(s)
            one = jnp.max(s, axis=0, keepdims=True)
            top = one if top is None else jnp.maximum(top, one)
        top = jnp.maximum(top, FLOOR)
        total = None
        acc = None
        for b in range(count):
            w = jnp.exp2((parts[b] - top) * base)
            one = jnp.sum(w, axis=0, keepdims=True)
            total = one if total is None else total + one
            wb = w.astype(jnp.bfloat16)
            p_ref[0, b] = wb
            out = dot(kv_ref[b, :, dim:], wb, TN)
            acc = out if acc is None else acc + out
        o_ref[0] = acc
        do_t = do.astype(jnp.float32).T
        delta = jnp.sum(acc * do_t, axis=0, keepdims=True)
        safe = jnp.maximum(total, 1e-30)
        st_ref[0, 0:1, :] = top * base + jnp.log2(safe)
        st_ref[0, 1:2, :] = delta / safe
        st_ref[0, 2:3, :] = top * base

    for g in range(groups):
        pl.when(zh == g)(lambda g=g: run(g + 1))


def backward_kernel(zh_ref, qd_ref, kv_ref, p_ref, o_ref, st_ref, all_ref, y_ref, z_ref, dk_ref, dv_ref):
    j = pl.program_id(0)
    rows = z_ref.shape[1]
    dim = o_ref.shape[1]
    groups = kv_ref.shape[0]
    scale = 1.0 / math.sqrt(dim)
    zh = zh_ref[0]

    @pl.when(j == 0)
    def _():
        dk_ref[...] = jnp.zeros_like(dk_ref)
        dv_ref[...] = jnp.zeros_like(dv_ref)

    q = qd_ref[0, :rows, :dim]
    do = qd_ref[0, :rows, dim:]
    lses = all_ref[:, 0, 0, :]
    tops = jnp.max(lses, axis=0, keepdims=True)
    fac = jnp.exp2(lses - tops)
    total = jnp.sum(fac, axis=0, keepdims=True)
    delta = jnp.sum(fac * all_ref[:, 0, 1, :], axis=0, keepdims=True) / total
    lse = tops + jnp.log2(total)
    c = jnp.exp2(st_ref[0, 2:3, :] - lse)
    y_ref[0, :dim, :] = (o_ref[0] * c).astype(jnp.bfloat16)

    def run(count):
        acc = None
        for b in range(count):
            k = kv_ref[b, :, :dim]
            dp = dot(kv_ref[b, :, dim:], do, NT)
            chance = p_ref[0, b].astype(jnp.float32) * c
            ds = (chance * (dp - delta)).astype(jnp.bfloat16)
            dv_ref[b] += dot(chance.astype(jnp.bfloat16), do, NN)
            dk_ref[b] += dot(ds, q, NN)
            out = dot(k, ds, TN)
            acc = out if acc is None else acc + out
        y_ref[0, dim:, :] = (acc * scale).astype(jnp.bfloat16)

    for g in range(groups):
        pl.when(zh == g)(lambda g=g: run(g + 1))

    @pl.when(j == pl.num_programs(0) - 1)
    def _():
        z_ref[:, :, :dim] = (dk_ref[...] * scale).astype(jnp.bfloat16)
        z_ref[:, :, dim:] = dv_ref[...].astype(jnp.bfloat16)


def forward(zh, qd, kv, sid):
    ny, packed, wide = qd.shape
    nz, rows, _ = kv.shape
    dim = wide // 2
    flops = 2 * 2 * ny * rows * nz * rows * dim
    return pl.pallas_call(
        forward_kernel,
        grid_spec=pltpu.PrefetchScalarGridSpec(
            num_scalar_prefetch=1,
            grid=(ny,),
            in_specs=[
                pl.BlockSpec((1, packed, wide), lambda j, z: (j, 0, 0)),
                pl.BlockSpec((nz, rows, wide), lambda j, z: (0, 0, 0)),
                pl.BlockSpec((rows, 128), lambda j, z: (0, 0)),
            ],
            out_specs=[
                pl.BlockSpec((1, nz, rows, rows), lambda j, z: (j, 0, 0, 0)),
                pl.BlockSpec((1, dim, rows), lambda j, z: (j, 0, 0)),
                pl.BlockSpec((1, 8, rows), lambda j, z: (j, 0, 0)),
            ],
        ),
        out_shape=[
            jax.ShapeDtypeStruct((ny, nz, rows, rows), jnp.bfloat16),
            jax.ShapeDtypeStruct((ny, dim, rows), jnp.float32),
            jax.ShapeDtypeStruct((ny, 8, rows), jnp.float32),
        ],
        cost_estimate=pl.CostEstimate(flops=flops, transcendentals=ny * nz * rows * rows, bytes_accessed=8 << 20),
        name="attend",
    )(zh, qd, kv, sid)


def backward(zh, qd, kv, p, o, st, all_st):
    ny, packed, wide = qd.shape
    nz, rows, _ = kv.shape
    dim = wide // 2
    flops = 4 * 2 * ny * rows * nz * rows * dim
    return pl.pallas_call(
        backward_kernel,
        grid_spec=pltpu.PrefetchScalarGridSpec(
            num_scalar_prefetch=1,
            grid=(ny,),
            in_specs=[
                pl.BlockSpec((1, packed, wide), lambda j, z: (j, 0, 0)),
                pl.BlockSpec((nz, rows, wide), lambda j, z: (0, 0, 0)),
                pl.BlockSpec((1, nz, rows, rows), lambda j, z: (j, 0, 0, 0)),
                pl.BlockSpec((1, dim, rows), lambda j, z: (j, 0, 0)),
                pl.BlockSpec((1, 8, rows), lambda j, z: (j, 0, 0)),
                pl.BlockSpec((ny, 1, 2, rows), lambda j, z: (0, j, 0, 0)),
            ],
            out_specs=[
                pl.BlockSpec((1, wide, rows), lambda j, z: (j, 0, 0)),
                pl.BlockSpec((nz, rows, wide), lambda j, z: (0, 0, 0)),
            ],
            scratch_shapes=[
                pltpu.VMEM((nz, rows, dim), jnp.float32),
                pltpu.VMEM((nz, rows, dim), jnp.float32),
            ],
        ),
        out_shape=[
            jax.ShapeDtypeStruct((ny, wide, rows), jnp.bfloat16),
            jax.ShapeDtypeStruct((nz, rows, wide), jnp.bfloat16),
        ],
        cost_estimate=pl.CostEstimate(flops=flops, transcendentals=0, bytes_accessed=8 << 20),
        name="attend_back",
    )(zh, qd, kv, p, o, st, all_st)


def to_all(x, axis, count):
    return lax.all_to_all(jnp.broadcast_to(x[None], (count,) + x.shape), axis, 0, 0, tiled=True)


def on_device(queries, key_rows, values, out_grad, query_gain, key_gain, stretch_id):
    rows, dim = queries.shape
    nz, ny = lax.axis_size("z_hi"), lax.axis_size("y")
    ns = lax.axis_size("z_lo") * lax.axis_size("x") * lax.axis_size("core")
    width = dim * ns
    zh = lax.axis_index("z_hi").astype(jnp.int32).reshape(1)
    query_wide = queries.astype(jnp.float32)
    key_wide = key_rows.astype(jnp.float32)
    squares = jnp.stack([jnp.sum(query_wide * query_wide, axis=1), jnp.sum(key_wide * key_wide, axis=1)])
    squares = jnp.sum(to_all(squares, SECTION, ns), axis=0)
    roots = lax.rsqrt(squares / width + EPSILON)
    query_root, key_root = roots[0], roots[1]
    query_hat = (query_wide * query_root[:, None] * query_gain[None, :]).astype(jnp.bfloat16)
    key_hat = (key_wide * key_root[:, None] * key_gain[None, :]).astype(jnp.bfloat16)
    sid_row = jnp.broadcast_to(stretch_id.astype(jnp.bfloat16)[None, :], (EXTRA, rows))
    packed = jnp.concatenate([jnp.concatenate([query_hat, out_grad], axis=1), sid_row], axis=0)
    qd = to_all(packed, "y", ny)
    kv = lax.all_gather(jnp.concatenate([key_hat, values], axis=1), "z_hi", axis=0)
    sid = jnp.broadcast_to(stretch_id.astype(jnp.float32)[:, None], (rows, 128))
    p, o, st = forward(zh, qd, kv, sid)
    all_st = to_all(st[:, :2, :], "y", ny)
    all_st = all_st.reshape(ny, ny, 2, rows)
    to_y, to_z = backward(zh, qd, kv, p, o, st, all_st)
    got_y = lax.all_to_all(to_y, "y", 0, 0, tiled=True)
    got_z = lax.all_to_all(to_z, "z_hi", 0, 0, tiled=True)
    sum_y = jnp.sum(got_y.astype(jnp.float32), axis=0)
    sum_z = jnp.sum(got_z.astype(jnp.float32), axis=0)
    attended = sum_y[:dim].T.astype(jnp.bfloat16)
    query_grad = sum_y[dim:].T
    key_grad = sum_z[:, :dim]
    value_grad = sum_z[:, dim:]
    terms = jnp.stack(
        [
            jnp.sum(query_grad * query_gain[None, :] * query_wide, axis=1),
            jnp.sum(key_grad * key_gain[None, :] * key_wide, axis=1),
        ]
    )
    terms = jnp.sum(to_all(terms, SECTION, ns), axis=0)
    grad_queries = (
        query_gain[None, :] * query_root[:, None] * query_grad
        - query_wide * (query_root**3 * terms[0] / width)[:, None]
    )
    grad_keys = (
        key_gain[None, :] * key_root[:, None] * key_grad
        - key_wide * (key_root**3 * terms[1] / width)[:, None]
    )
    return (attended, grad_queries, grad_keys, value_grad)


def solution(mesh):
    fine = Mesh(mesh.devices.reshape(3, 4, 2, 4, 8), SECTION + SEQ)
    full = P(SEQ, SECTION)
    return jax.shard_map(
        on_device,
        mesh=fine,
        in_specs=(full, full, full, full, P(SECTION), P(SECTION), P(SEQ)),
        out_specs=(full, full, full, full),
        check_vma=False,
    )
```

time: 594 us -> 175 us (0.29)
  blocking collectives: 346 us -> 76.9 us
  waiting for transfers between devices: 136 us -> 40 us
  matrix products: 79.7 us -> 0 us
  starting transfers between devices: 0.16 us -> 27 us
  Pallas kernels: 0 us -> 17.2 us
  between operations: 14 us -> 0.83 us
  local copies, waits for them, and re-layouts: 0.42 us -> 7.88 us
    all_gather x3 -> x1, blocking collectives: 220 us -> 29.1 us  [on_device(): lax.all_gather(jnp.concatenate([key_hat, values], axis=1), 'z_hi', axis=0)]
    all_gather x4 -> x0, waiting for transfers between devices: 135 us -> none  [the longest x1 99.1 us: on_device(): lax.all_gather(values, 'seq', axis=0, tiled=True)]
    psum x2 -> x0, blocking collectives: 126 us -> none  [the longest x1 70.3 us: on_device(): lax.psum((jnp.sum(query_grad * query_gain[None, :] * query_wide, axis=1),...]
    dot_general x56 -> x0, matrix products: 79.7 us -> none  [the longest x8 13.8 us: key_side_update(): jnp.einsum('tu,td->ud', grad_scores, query_part, preferred_element_type=j...]
    all_to_all x0 -> x2, blocking collectives: none -> 47.8 us  [the longest x1 35.9 us: on_device(): got_z = lax.all_to_all(to_z, 'z_hi', 0, 0, tiled=True)]
    all_to_all x0 -> x4, waiting for transfers between devices: none -> 40 us  [the longest x1 27.2 us: on_device(): got_y = lax.all_to_all(to_y, 'y', 0, 0, tiled=True)]
    all_to_all x0 -> x4, starting transfers between devices: none -> 27 us  [the longest x3 23.3 us: to_all(): lax.all_to_all(jnp.broadcast_to(x[None], (count,) + x.shape), axis, 0, 0,...]
    pallas_call x0 -> x2, Pallas kernels: none -> 17.2 us  [the longest x1 8.74 us: backward(): pl.pallas_call(backward_kernel, grid_spec=pltpu.PrefetchScalarGridSpec(nu...]
  transfers between devices with their start and end apart: 4 -> 4, of which waited for: 3 -> 4; matrix products, arithmetic and copies ran while one was open for 8% -> 2% of each run, Pallas kernels for 0% -> 0%
where the time goes in v1:
time: 175 us; the launch traced here: 174 us
  blocking collectives  76.9 us (44%)
  waiting for transfers between devices  40 us (23%)
  starting transfers between devices  27 us (15%)
  Pallas kernels  17.2 us (10%)
  local copies, waits for them, and re-layouts  7.88 us (5%)
  other arithmetic  4.06 us (2%)
    all_to_all x1, blocking collectives, on_device(): got_z = lax.all_to_all(to_z, 'z_hi', 0, 0, tiled=True)  35.9 us
    all_gather x1, blocking collectives, on_device(): lax.all_gather(jnp.concatenate([key_hat, values], axis=1), 'z_hi', axis=0)  29.1 us
    all_to_all x1, waiting for transfers between devices, on_device(): got_y = lax.all_to_all(to_y, 'y', 0, 0, tiled=True)  27.2 us
    all_to_all x3, starting transfers between devices, to_all(): lax.all_to_all(jnp.broadcast_to(x[None], (count,) + x.shape), axis, 0, 0,...  23.3 us
    all_to_all x3, waiting for transfers between devices, to_all(): lax.all_to_all(jnp.broadcast_to(x[None], (count,) + x.shape), axis, 0, 0,...  12.8 us
    all_to_all x1, blocking collectives, to_all(): lax.all_to_all(jnp.broadcast_to(x[None], (count,) + x.shape), axis, 0, 0,...  11.9 us
    pallas_call x1, Pallas kernels, backward(): pl.pallas_call(backward_kernel, grid_spec=pltpu.PrefetchScalarGridSpec(nu...  8.74 us
    pallas_call x1, Pallas kernels, forward(): pl.pallas_call(forward_kernel, grid_spec=pltpu.PrefetchScalarGridSpec(num...  8.41 us
  transfers between devices with their start and end apart: 4, of which 4 were waited for; matrix products, arithmetic and copies ran while one was open for 2% of the time, Pallas kernels for 0%

profile of v1, /device:TPU:1, one launch (start us, length us, event | category | flops | bytes accessed | tf_op | source)
XLA Modules:
  0.0 173.8 jit_solution(326585687426870342)
XLA Ops:
  0.6 1.0 fusion.5
  1.6 0.9 copy.21
  3.2 14.0 %all-to-all-start = ((f32[24,2,256]{2,1,0:T(2,128)}), f32[24,2,256]{2,1,0:T(2,128)S(1)}, u32[]{:S(2)}, u32[]{:S(2)}) async-start(f32[24,2,256]{2,1,0:T(2,128)} %broadcast_in_dim.12), calls=%async_computation | async-start | bytes 98304 | tf_op jit(solution)/shard_map/all_to_all | solution.py:184
  17.2 0.9 copy.23
  18.2 0.8 fusion.18
  18.9 5.3 %all-to-all-done = f32[24,2,256]{2,1,0:T(2,128)S(1)} async-done(((f32[24,2,256]{2,1,0:T(2,128)}), f32[24,2,256]{2,1,0:T(2,128)S(1)}, u32[]{:S(2)}, u32[]{:S(2)}) %all-to-all-start) | async-done | bytes 49184 | tf_op jit(solution)/shard_map/all_to_all | solution.py:184
  24.2 0.7 fusion.2
  25.3 1.1 broadcast_in_dim.14
  26.3 3.6 %all-to-all-start.1 = ((bf16[8,272,256]{2,1,0:T(8,128)(2,1)}), bf16[8,272,256]{2,1,0:T(8,128)(2,1)S(1)}, u32[]{:S(2)}, u32[]{:S(2)}) async-start(bf16[8,272,256]{2,1,0:T(8,128)(2,1)} %broadcast_in_dim.14), calls=%async_computation.1 | async-start | bytes 2228224 | tf_op jit(solution)/shard_map/all_to_all | solution.py:184
  30.1 29.1 %all-gather = bf16[1024,256]{1,0:T(8,128)(2,1)} all-gather(bf16[256,256]{1,0:T(8,128)(2,1)S(1)} %pad_maximum_fusion.1), channel_id=2, replica_groups=mesh['z_lo'=3,'x'=4,'core'=2,'z_hi'=4,'y'=8] {'z_hi'}, dimensions={0}, use_global_device_ids=true | all-gather | bytes 655360 | tf_op jit(solution)/shard_map/all_gather | solution.py:204
  59.2 1.3 all-to-all-done.1.qd_ref
  60.5 0.9 broadcast_in_dim.15.sid_ref
  61.5 8.4 %attend.1 = (bf16[8,4,256,256]{3,2,1,0:T(8,128)(2,1)}, f32[8,128,256]{2,1,0:T(8,128)}, f32[8,8,256]{2,1,0:T(8,128)}) custom-call(s32[1]{0:T(128)} %bitcast.zh_ref, bf16[8,272,256]{2,1,0:T(8,128)(2,1)} %copy-done, bf16[4,256,256]{2,1,0:T(8,128)(2,1)} %bitcast.18, f32[256,128]{1,0:T(8,128)} %broadcast_in_dim.15.sid_ref), custom_call_target="tpu_custom_call" | custom-call | flops 1073741824 | bytes 8388608 | tf_op jit(solution)/shard_map/attend/pallas_call | solution.py:121
  69.9 0.8 slice.30
  70.8 11.9 %all_to_all.30.all_ref = f32[8,8,2,256]{3,2,1,0:T(2,128)} all-to-all(f32[8,8,2,256]{3,2,1,0:T(2,128)S(1)} %broadcast_in_dim.16), channel_id=1, replica_groups=mesh['z_lo'=3,'x'=4,'core'=2,'z_hi'=4,'y'=8] {'y'}, dimensions={0} | all-to-all | bytes 262144 | tf_op jit(solution)/shard_map/all_to_all | solution.py:184
  82.7 8.7 %attend_back.1 = (bf16[8,256,256]{2,1,0:T(8,128)(2,1)}, bf16[4,256,256]{2,1,0:T(8,128)(2,1)}) custom-call(s32[1]{0:T(128)} %bitcast.zh_ref, bf16[8,272,256]{2,1,0:T(8,128)(2,1)} %copy-done, bf16[4,256,256]{2,1,0:T(8,128)(2,1)} %bitcast.19, bf16[8,4,256,256]{3,2,1,0:T(8,128)(2,1)} %get-tuple-element.9.p_ref, f32[8,128,256]{2,1,0:T(8,128)} %get-tuple-element.10.o_ref, ...), custom_call_target="tpu_custom_call" | custom-call | flops 2147483648 | bytes 8388608 | tf_op jit(solution)/shard_map/attend_back/pallas_call | solution.py:152
  91.5 35.9 %all_to_all.31 = bf16[4,256,256]{2,1,0:T(8,128)(2,1)S(1)} all-to-all(bf16[4,256,256]{2,1,0:T(8,128)(2,1)} %get-tuple-element.13), channel_id=1, replica_groups=mesh['z_lo'=3,'x'=4,'core'=2,'z_hi'=4,'y'=8] {'z_hi'}, dimensions={0} | all-to-all | bytes 1048576 | tf_op jit(solution)/shard_map/all_to_all | solution.py:211
  127.4 3.7 %all-to-all-start.3 = ((bf16[8,256,256]{2,1,0:T(8,128)(2,1)}), bf16[8,256,256]{2,1,0:T(8,128)(2,1)S(1)}, u32[]{:S(2)}, u32[]{:S(2)}) async-start(bf16[8,256,256]{2,1,0:T(8,128)(2,1)} %get-tuple-element.12), calls=%async_computation.3 | async-start | bytes 2097152 | tf_op jit(solution)/shard_map/all_to_all | solution.py:210
  131.2 27.2 %all-to-all-done.3 = bf16[8,256,256]{2,1,0:T(8,128)(2,1)S(1)} async-done(((bf16[8,256,256]{2,1,0:T(8,128)(2,1)}), bf16[8,256,256]{2,1,0:T(8,128)(2,1)S(1)}, u32[]{:S(2)}, u32[]{:S(2)}) %all-to-all-start.3) | async-done | bytes 1048608 | tf_op jit(solution)/shard_map/all_to_all | solution.py:210
  159.3 5.7 %all-to-all-start.5 = ((f32[24,2,256]{2,1,0:T(2,128)}), f32[24,2,256]{2,1,0:T(2,128)S(1)}, u32[]{:S(2)}, u32[]{:S(2)}) async-start(f32[24,2,256]{2,1,0:T(2,128)} %broadcast_in_dim.17), calls=%async_computation.5 | async-start | bytes 98304 | tf_op jit(solution)/shard_map/all_to_all | solution.py:184
  165.1 0.7 copy.26
  165.8 6.2 %all-to-all-done.5 = f32[24,2,256]{2,1,0:T(2,128)S(1)} async-done(((f32[24,2,256]{2,1,0:T(2,128)}), f32[24,2,256]{2,1,0:T(2,128)S(1)}, u32[]{:S(2)}, u32[]{:S(2)}) %all-to-all-start.5) | async-done | bytes 49184 | tf_op jit(solution)/shard_map/all_to_all | solution.py:184
  172.1 0.8 fusion.15
  173.0 0.8 copy.27
  (34 shorter events, 2.6 us)
Async XLA Ops:
  3.2 21.0 %all-to-all-start = ((f32[24,2,256]{2,1,0:T(2,128)}), f32[24,2,256]{2,1,0:T(2,128)S(1)}, u32[]{:S(2)}, u32[]{:S(2)}) async-start(f32[24,2,256]{2,1,0:T(2,128)} %broadcast_in_dim.12), calls=%async_computation | async-start | bytes 98304 | tf_op jit(solution)/shard_map/all_to_all | solution.py:184
  25.1 4.8 %copy-start.1 = (bf16[256,128]{1,0:T(8,128)(2,1)S(1)}, bf16[256,128]{1,0:T(8,128)(2,1)}, u32[]{:S(2)}) copy-start(bf16[256,128]{1,0:T(8,128)(2,1)} %param.8) | copy-start | bytes 196612
  25.1 4.8 %copy-start.4 = (f32[128]{0:T(128)S(1)}, f32[128]{0:T(128)}, u32[]{:S(2)}) copy-start(f32[128]{0:T(128)} %param.12) | copy-start | bytes 1540
  25.1 4.9 %copy-start.2 = (bf16[256,128]{1,0:T(8,128)(2,1)S(1)}, bf16[256,128]{1,0:T(8,128)(2,1)}, u32[]{:S(2)}) copy-start(bf16[256,128]{1,0:T(8,128)(2,1)} %param.9) | copy-start | bytes 196612
  26.3 34.1 %all-to-all-start.1 = ((bf16[8,272,256]{2,1,0:T(8,128)(2,1)}), bf16[8,272,256]{2,1,0:T(8,128)(2,1)S(1)}, u32[]{:S(2)}, u32[]{:S(2)}) async-start(bf16[8,272,256]{2,1,0:T(8,128)(2,1)} %broadcast_in_dim.14), calls=%async_computation.1 | async-start | bytes 2228224 | tf_op jit(solution)/shard_map/all_to_all | solution.py:184
  60.5 1.0 copy-start
  127.4 31.2 %copy-start.3 = (f32[128]{0:T(128)S(1)}, f32[128]{0:T(128)}, u32[]{:S(2)}) copy-start(f32[128]{0:T(128)} %param.11) | copy-start | bytes 1540
  127.4 31.1 %all-to-all-start.3 = ((bf16[8,256,256]{2,1,0:T(8,128)(2,1)}), bf16[8,256,256]{2,1,0:T(8,128)(2,1)S(1)}, u32[]{:S(2)}, u32[]{:S(2)}) async-start(bf16[8,256,256]{2,1,0:T(8,128)(2,1)} %get-tuple-element.12), calls=%async_computation.3 | async-start | bytes 2097152 | tf_op jit(solution)/shard_map/all_to_all | solution.py:210
  159.3 12.7 %all-to-all-start.5 = ((f32[24,2,256]{2,1,0:T(2,128)}), f32[24,2,256]{2,1,0:T(2,128)S(1)}, u32[]{:S(2)}, u32[]{:S(2)}) async-start(f32[24,2,256]{2,1,0:T(2,128)} %broadcast_in_dim.17), calls=%async_computation.5 | async-start | bytes 98304 | tf_op jit(solution)/shard_map/all_to_all | solution.py:184
